TPU v7x, 32 devices: a whole 2x2x4 slice. The times are simulated.
32 devices in a mesh: grp: 2 (over x), ctx: 16 (over z, y, core).
Axes of the slice: x: 2, y: 2, z: 4, core: 2. Of those that a mesh axis runs over, the one named last changes fastest.
Arguments:
- queries: bfloat16 [960, 4096], P(None, ('grp', 'ctx')), parts along dimension 1, may hold values from -6 to 6
- key_rows: bfloat16 [960, 4096], P(None, ('grp', 'ctx')), parts along dimension 1, may hold values from -6 to 6
- value_rows: bfloat16 [960, 4096], P(None, ('grp', 'ctx')), parts along dimension 1, may hold values from -6 to 6
- short_taps: float32 [3, 960, 7], replicated, may hold values from -2 to 2
- long_filter: bfloat16 [960, 2048], P('ctx'), may hold values from -0.125 to 0.125
Outputs:
- mixed: bfloat16 [960, 4096], P(None, ('grp', 'ctx')), parts along dimension 1
There are 2 independent parts, one for each index of `grp`. A program takes and returns all parts, laid end to end along the dimension named above; an argument that names none is the same for every part. Nothing has to cross between parts.
All inputs are finite; a program needn't handle non-finite values.
Results may differ from a plain program's by a relative error of at most 0.0057.
Values may be sent and summed in bfloat16 or wider, within the bound.
A program may use at most 64 MiB of HBM per device.

v0:
```python
import math
import jax
import jax.numpy as jnp
from jax import lax
from jax.sharding import PartitionSpec as P

TAPS = 7
precise = lax.Precision.HIGH


def with_halo(value, sides, width):
    for axis, dim in sides:
        size, length = (lax.axis_size(axis), value.shape[dim])
        up = [(i, (i + 1) % size) for i in range(size - 1)]
        down = [(j, i) for i, j in up]
        last = lax.slice_in_dim(value, length - width, length, axis=dim)
        leading = lax.slice_in_dim(value, 0, width, axis=dim)
        before = lax.ppermute(last, axis, up)
        after = lax.ppermute(leading, axis, down)
        value = jnp.concatenate([before, value, after], axis=dim)
    return value


def angles(count_rows, count_cols, modulus):
    row_ids = lax.broadcasted_iota(jnp.int32, (count_rows, count_cols), 0)
    col_ids = lax.broadcasted_iota(jnp.int32, (count_rows, count_cols), 1)
    phase = (row_ids * col_ids % modulus).astype(jnp.float32) * (2.0 * math.pi / modulus)
    return (jnp.cos(phase), jnp.sin(phase))


def fourier_tables(length):
    inner_len = min(128, length)
    padded_len = 2 * length
    outer_len = padded_len // inner_len
    cos_outer, sin_outer = angles(outer_len // 2, outer_len, outer_len)
    cos_twist, sin_twist = angles(outer_len, inner_len, padded_len)
    cos_inner, sin_inner = angles(inner_len, inner_len, inner_len)
    outer_fwd = jnp.stack([cos_outer, -sin_outer])
    inner_fwd = jnp.stack([jnp.stack([cos_inner, -sin_inner]), jnp.stack([sin_inner, cos_inner])])
    inner_inv = jnp.stack([jnp.stack([cos_inner, sin_inner]), jnp.stack([-sin_inner, cos_inner])])
    return (outer_fwd, cos_twist, sin_twist, inner_fwd, inner_inv, padded_len)


def forward(signal, tables):
    outer_fwd, cos_twist, sin_twist, inner_fwd, inner_inv, padded_len = tables
    shaped = signal.reshape(signal.shape[:-1] + (outer_fwd.shape[1], inner_fwd.shape[2]))
    first = jnp.einsum("...ab,caf->...cfb", shaped, outer_fwd, precision=precise)
    first_real = first[..., 0, :, :]
    first_imag = first[..., 1, :, :]
    twist = jnp.stack(
        [
            first_real * cos_twist + first_imag * sin_twist,
            first_imag * cos_twist - first_real * sin_twist,
        ],
        axis=-3,
    )
    return jnp.einsum("...cfb,cdbk->...dfk", twist, inner_fwd, precision=precise)


def inverse(spectrum, tables):
    outer_fwd, cos_twist, sin_twist, inner_fwd, inner_inv, padded_len = tables
    first = jnp.einsum("...cfk,cdkb->...dfb", spectrum, inner_inv, precision=precise)
    first_real = first[..., 0, :, :]
    first_imag = first[..., 1, :, :]
    twist = jnp.stack(
        [
            first_real * cos_twist - first_imag * sin_twist,
            first_imag * cos_twist + first_real * sin_twist,
        ],
        axis=-3,
    )
    result = jnp.einsum("...cfb,caf->...ab", twist, outer_fwd, precision=precise)
    result = result / padded_len
    return result.reshape(result.shape[:-2] + (result.shape[-2] * result.shape[-1],))


def on_device(queries, key_rows, value_rows, short_taps, long_filter):
    tokens = queries.shape[1]
    rim_width = TAPS - 1
    stacked = jnp.stack([queries, key_rows, value_rows])
    padded = with_halo(stacked, (("ctx", 2),), rim_width)
    mirrored_taps = short_taps[:, ::-1, :]
    causal = jnp.zeros(stacked.shape, jnp.float32)
    anticausal = jnp.zeros(stacked.shape, jnp.float32)
    for offset in range(TAPS):
        begin = rim_width - offset
        causal = causal + short_taps[:, :, offset, None] * padded[:, :, begin : begin + tokens]
        later = rim_width + offset
        anticausal = (
            anticausal + mirrored_taps[:, :, offset, None] * padded[:, :, later : later + tokens]
        )
    product_a = (causal[1] * causal[2]).astype(jnp.bfloat16)
    product_b = (anticausal[1] * anticausal[2]).astype(jnp.bfloat16)
    tables = fourier_tables(long_filter.shape[1])
    outgoing = jnp.stack([product_a, product_b[::-1]])
    channel_rows = lax.all_to_all(outgoing, "ctx", split_axis=1, concat_axis=2, tiled=True)
    filter_spec = forward(long_filter.astype(jnp.float32), tables)
    data_spec = forward(channel_rows.astype(jnp.float32), tables)
    filter_real = filter_spec[:, 0]
    filter_imag = filter_spec[:, 1]
    data_real = data_spec[:, :, 0]
    data_imag = data_spec[:, :, 1]
    first_real = filter_real * data_real[0] - filter_imag * data_imag[0]
    first_imag = filter_real * data_imag[0] + filter_imag * data_real[0]
    second_real = filter_real * data_real[1] + filter_imag * data_imag[1]
    second_imag = filter_real * data_imag[1] - filter_imag * data_real[1]
    spectrum = jnp.stack(
        [jnp.stack([first_real, first_imag], axis=1), jnp.stack([second_real, second_imag], axis=1)]
    )
    convolved = inverse(spectrum, tables).astype(jnp.bfloat16)
    token_rows = lax.all_to_all(convolved, "ctx", split_axis=2, concat_axis=1, tiled=True)
    mixed_b = token_rows[1][::-1]
    result = causal[0] * token_rows[0].astype(jnp.float32) + anticausal[0] * mixed_b.astype(
        jnp.float32
    )
    return result.astype(jnp.bfloat16)


def solution(mesh):
    placed = (
        P(None, ("grp", "ctx")),
        P(None, ("grp", "ctx")),
        P(None, ("grp", "ctx")),
        P(),
        P("ctx", None),
    )
    return jax.shard_map(
        on_device, mesh=mesh, in_specs=placed, out_specs=P(None, ("grp", "ctx")), check_vma=False
    )
```

profile of v0, /device:TPU:0, one launch (start us, length us, event | category | flops | bytes accessed | tf_op | source)
XLA Modules:
  0.0 102.4 jit_solution(13261690223920789769)
XLA Ops:
  0.0 1.3 %pad_maximum_fusion.2 = bf16[3,960,128]{2,1,0:T(8,128)(2,1)S(1)} fusion(bf16[1,960,128]{2,1,0:T(8,128)(2,1)} %bitcast.184, bf16[1,960,128]{2,1,0:T(8,128)(2,1)} %bitcast.188, bf16[1,960,128]{2,1,0:T(8,128)(2,1)} %bitcast.192), kind=kLoop, calls=%fused_computation.55 | loop fusion | flops 737280 | bytes 1474560 | tf_op jit(solution)/shard_map/stack | solution.py:80
  1.3 0.3 fusion.94
  1.6 0.3 copy.51
  1.9 1.3 %collective-permute-start.1 = (bf16[3,960,6]{1,2,0:T(8,128)(2,1)S(1)}, bf16[3,960,6]{1,2,0:T(8,128)(2,1)S(1)}, u32[]{:S(2)}, u32[]{:S(2)}) collective-permute-start(bf16[3,960,6]{1,2,0:T(8,128)(2,1)S(1)} %copy.51), channel_id=1, source_target_pairs={{1,0},{2,1},{3,2},{4,3},{5,4},{6,5},{7,6},{8,7},{9,8},{10,9},{11,1... | collective-permute-start | bytes 103688 | tf_op jit(solution)/shard_map/ppermute | solution.py:19
  3.2 0.3 copy.47
  3.5 3.0 %collective-permute-start = (bf16[3,960,6]{1,2,0:T(8,128)(2,1)S(1)}, bf16[3,960,6]{1,2,0:T(8,128)(2,1)S(1)}, u32[]{:S(2)}, u32[]{:S(2)}) collective-permute-start(bf16[3,960,6]{1,2,0:T(8,128)(2,1)S(1)} %copy.47), channel_id=1, source_target_pairs={{0,1},{1,2},{2,3},{3,4},{4,5},{5,6},{6,7},{7,8},{8,9},{9,10},{10,1... | collective-permute-start | bytes 103688 | tf_op jit(solution)/shard_map/ppermute | solution.py:18
  6.6 0.3 fusion.70
  6.9 0.3 fusion.68
  7.3 0.7 reverse.8
  8.0 0.1 slice.344
  8.1 0.7 reverse.7
  8.9 0.1 slice.343
  9.0 0.7 reverse.12
  9.7 0.1 slice.348
  9.8 0.6 copy_bitcast_fusion.11
  10.4 0.7 reverse.11
  11.1 0.1 slice.347
  11.2 0.7 reverse.10
  12.0 0.1 slice.346
  12.1 0.6 copy_bitcast_fusion.9
  12.7 0.7 reverse.9
  13.5 0.6 copy_bitcast_fusion
  14.1 0.6 copy_bitcast_fusion.4
  14.7 0.6 copy_bitcast_fusion.2
  15.4 0.7 fusion.60
  16.1 0.6 copy.140
  16.7 0.7 reverse.13
  17.5 0.1 slice.349
  17.6 0.6 copy.139
  18.2 0.4 copy.48
  18.7 1.2 %copy.52 = bf16[3,960,6]{2,1,0:T(8,128)(2,1)} copy(bf16[3,960,6]{1,2,0:T(8,128)(2,1)S(1)} %collective-permute-done.1) | data formatting | bytes 69120 | tf_op jit(solution)/shard_map/ppermute | solution.py:19
  19.9 2.5 %maximum_maximum_fusion = (bf16[3,960,134]{2,1,0:T(8,128)(2,1)S(1)}, bf16[3,960,134]{2,1,0:T(8,128)(2,1)S(1)}) fusion(bf16[1,960,128]{2,1,0:T(8,128)(2,1)S(1)} %bitcast.185, bf16[1,960,128]{2,1,0:T(8,128)(2,1)S(1)} %bitcast.189, bf16[1,960,128]{2,1,0:T(8,128)(2,1)S(1)} %bitcast.193, bf16[3,960,6]{2,1,0:T(8,128)(2,1)S(1)} %copy.48, bf16[3,960,6]{2,1,0:T(8,128)(2,1)} %copy.52), kind=kLoop, calls=%fused_computation.39 | loop fusion | flops 6174720 | bytes 2350080 | tf_op jit(solution)/shard_map/concatenate | solution.py:20
  22.6 4.5 %fusion.31 = f32[3,960,128]{2,1,0:T(8,128)S(1)} fusion(bf16[3,960,134]{2,1,0:T(8,128)(2,1)S(1)} %get-tuple-element.16, f32[3,960]{1,0:T(4,128)S(1)} %copy-done.13, f32[3,960]{1,0:T(4,128)S(1)} %copy-done.14, f32[3,960]{1,0:T(4,128)S(1)} %copy-done.17, f32[3,960]{1,0:T(4,128)S(1)} %copy-done.18, f32[3,960]{1,0:T(4,128)S(1)} %copy-done.15, ...), kind=kLoop, calls=%fused_computation.38 | loop fusion | flops 8110080 | bytes 6716160 | tf_op jit(solution)/shard_map/add | solution.py:90
  27.1 1.1 %copy-done = f32[3,960,128]{2,1,0:T(8,128)} copy-done((f32[3,960,128]{2,1,0:T(8,128)}, f32[3,960,128]{2,1,0:T(8,128)S(1)}, u32[]{:S(2)}) %copy-start) | copy-done | bytes 1474584
  28.3 0.6 rev.7
  29.0 4.3 %fusion.25 = f32[3,960,128]{2,1,0:T(8,128)S(1)} fusion(bf16[3,960,134]{2,1,0:T(8,128)(2,1)S(1)} %get-tuple-element.15, f32[3,960]{1,0:T(4,128)S(1)} %get-tuple-element.34, f32[3,960]{1,0:T(4,128)S(1)} %get-tuple-element.35, f32[3,960]{1,0:T(4,128)S(1)} %copy-done.11, f32[3,960]{1,0:T(4,128)S(1)} %copy-done.12, f32[3,960]{1,0:T(4,128)S(1)} %copy-done.9, ...), kind=kLoop, calls=%fused_computation.32 | loop fusion | flops 8110080 | bytes 6716160 | tf_op jit(solution)/shard_map/add | solution.py:87
  33.3 1.1 %copy-done.1 = f32[3,960,128]{2,1,0:T(8,128)} copy-done((f32[3,960,128]{2,1,0:T(8,128)}, f32[3,960,128]{2,1,0:T(8,128)S(1)}, u32[]{:S(2)}) %copy-start.1) | copy-done | bytes 1474584
  34.5 1.3 %copy.53 = bf16[2,960,128]{2,0,1:T(2,128)(2,1)} copy(bf16[2,960,128]{2,1,0:T(8,128)(2,1)S(1)} %pad_maximum_fusion.3) | data formatting | bytes 983040 | tf_op jit(solution)/shard_map/stack | solution.py:95
  35.8 8.1 %all-to-all-start = ((bf16[2,960,128]{2,0,1:T(2,128)(2,1)}), bf16[2,960,128]{2,0,1:T(2,128)(2,1)S(1)}, u32[]{:S(2)}, u32[]{:S(2)}) async-start(bf16[2,960,128]{2,0,1:T(2,128)(2,1)} %copy.53), calls=%async_computation | async-start | bytes 983040 | tf_op jit(solution)/shard_map/all_to_all | solution.py:96
  44.0 0.7 convolution_bitcast_fusion.1
  44.7 0.3 multiply_add_fusion.4
  45.0 0.2 pad_maximum_fusion
  45.2 2.0 %fusion.17 = f32[60,2,32,128]{3,0,2,1:T(8,128)S(1)} fusion(f32[60,2,32,128]{3,2,0,1:T(8,128)S(1)} %pad_maximum_fusion, f32[1,2,128,128]{3,2,0,1:T(8,128)S(1)} %get-tuple-element.22, f32[1,2,128,128]{3,2,0,1:T(8,128)S(1)} %get-tuple-element.32), kind=kOutput, calls=%fused_computation.25 | convolution fusion | flops 755040256 | bytes 4194304 | tf_op jit(solution)/shard_map/...cfb,cdbk->...dfk/dot_general | solution.py:57
  47.2 10.4 %all-to-all-done = bf16[2,960,128]{2,0,1:T(2,128)(2,1)S(1)} async-done(((bf16[2,960,128]{2,0,1:T(2,128)(2,1)}), bf16[2,960,128]{2,0,1:T(2,128)(2,1)S(1)}, u32[]{:S(2)}, u32[]{:S(2)}) %all-to-all-start) | async-done | bytes 491552 | tf_op jit(solution)/shard_map/all_to_all | solution.py:96
  57.6 1.2 %convolution_bitcast_fusion = f32[2,60,2,32,128]{4,3,1,0,2:T(8,128)S(1)} fusion(bf16[2,16,60,128]{3,0,2,1:T(2,128)(2,1)S(1)} %bitcast.196, f32[1,16,32]{2,1,0:T(8,128)S(1)} %get-tuple-element.46, f32[1,16,32]{2,1,0:T(8,128)S(1)} %get-tuple-element.47), kind=kOutput, calls=%fused_computation.17 | convolution fusion | flops 94372864 | bytes 4427776 | tf_op jit(solution)/shard_map/...ab,caf->...cfb/dot_general | solution.py:47
  58.8 0.8 multiply_add_fusion.1
  59.6 0.4 maximum_bitcast_fusion.1
  60.0 5.0 %fusion.8 = f32[2,60,2,32,128]{4,1,3,2,0:T(8,128)S(1)} fusion(f32[2,60,2,32,128,1]{4,3,1,0,2,5:T(8,128)S(1)} %maximum_bitcast_fusion.1, f32[1,2,128,128]{3,2,0,1:T(8,128)S(1)} %get-tuple-element.22, f32[1,2,128,128]{3,2,0,1:T(8,128)S(1)} %get-tuple-element.32), kind=kOutput, calls=%fused_computation.10 | convolution fusion | flops 1510014976 | bytes 8126464 | tf_op jit(solution)/shard_map/...cfb,cdbk->...dfk/dot_general | solution.py:57
  65.0 1.0 multiply_subtract_fusion.3
  65.9 0.1 maximum_bitcast_fusion.2
  66.1 0.2 maximum_bitcast_fusion.3
  66.4 0.4 maximum_bitcast_fusion
  66.8 0.4 copy-done.6
  67.3 4.5 %fusion.14 = f32[2,60,2,32,128]{4,3,1,0,2:T(8,128)S(1)} fusion(f32[2,60,2,32,128,1]{4,1,3,2,0,5:T(8,128)S(1)} %maximum_bitcast_fusion, f32[1,2,128,128]{3,2,1,0:T(8,128)S(1)} %copy-done.7, f32[1,2,128,128]{3,2,1,0:T(8,128)S(1)} %copy-done.6), kind=kOutput, calls=%fused_computation.16 | convolution fusion | flops 1510014976 | bytes 8126464 | tf_op jit(solution)/shard_map/...cfk,cdkb->...dfb/dot_general | solution.py:62
  71.8 0.6 multiply_subtract_fusion
  72.4 1.3 %fusion.41 = bf16[2,60,16,128]{3,2,1,0:T(8,128)(2,1)S(1)} fusion(f32[2,60,1,32,128]{4,3,1,0,2:T(8,128)S(1)} %get-tuple-element.10, f32[2,60,1,32,128]{4,3,1,0,2:T(8,128)S(1)} %get-tuple-element.9, f32[1,16,32]{2,1,0:T(8,128)S(1)} %get-tuple-element.46, f32[1,16,32]{2,1,0:T(8,128)S(1)} %get-tuple-element.47), kind=kOutput, calls=%fused_computation.44 | convolution fusion | flops 95847424 | bytes 4427776 | tf_op jit(solution)/shard_map/...cfb,caf->...ab/dot_general | solution.py:72
  73.7 0.8 copy.89
  74.6 2.8 %reshape.225 = bf16[16,2,7680]{2,1,0:T(2,128)(2,1)S(1)} reshape(bf16[2048,2,60]{2,1,0:T(2,128)(2,1)S(1)} %bitcast.182) | data formatting | bytes 983040
  77.4 17.7 %all_to_all.30 = bf16[16,2,7680]{2,1,0:T(2,128)(2,1)S(1)} all-to-all(bf16[16,2,7680]{2,1,0:T(2,128)(2,1)S(1)} %reshape.225), channel_id=1, replica_groups=mesh['grp'=2,'ctx'=16] {'ctx'}, dimensions={0} | all-to-all | bytes 983040 | tf_op jit(solution)/shard_map/all_to_all | solution.py:111
  95.0 3.5 %reshape.226 = bf16[2048,2,60]{2,1,0:T(2,128)(2,1)S(1)} reshape(bf16[16,2,7680]{2,1,0:T(2,128)(2,1)S(1)} %all_to_all.30) | data formatting | bytes 983040
  98.6 0.8 copy.88
  99.6 0.6 rev.8
  100.2 0.2 copy.64
  100.4 2.0 %fusion.46 = bf16[960,128]{1,0:T(8,128)(2,1)} fusion(f32[3,960,128]{2,1,0:T(8,128)} %copy-done, f32[960,128]{1,0:T(8,128)S(1)} %reshape.208, f32[3,960,128]{2,1,0:T(8,128)} %copy-done.1, bf16[960,128]{1,0:T(8,128)(2,1)S(1)} %rev.8), kind=kLoop, calls=%fused_computation.59 | loop fusion | flops 614400 | bytes 1966080 | tf_op jit(solution)/shard_map/convert_element_type | solution.py:116
  (54 shorter events, 0.9 us)
Async XLA Ops:
  1.3 5.9 %copy-start.8 = (f32[3,960,7]{1,2,0:T(8,128)S(1)}, f32[3,960,7]{1,2,0:T(8,128)}, u32[]{:S(2)}) copy-start(f32[3,960,7]{1,2,0:T(8,128)} %param.8) | copy-start | bytes 241924
  1.6 16.6 %copy-start.5 = (bf16[60,2048]{1,0:T(8,128)(2,1)S(1)}, bf16[60,2048]{1,0:T(8,128)(2,1)}, u32[]{:S(2)}) copy-start(bf16[60,2048]{1,0:T(8,128)(2,1)} %param.9) | copy-start | bytes 737284
  1.9 16.8 %collective-permute-start.1 = (bf16[3,960,6]{1,2,0:T(8,128)(2,1)S(1)}, bf16[3,960,6]{1,2,0:T(8,128)(2,1)S(1)}, u32[]{:S(2)}, u32[]{:S(2)}) collective-permute-start(bf16[3,960,6]{1,2,0:T(8,128)(2,1)S(1)} %copy.51), channel_id=1, source_target_pairs={{1,0},{2,1},{3,2},{4,3},{5,4},{6,5},{7,6},{8,7},{9,8},{10,9},{11,1... | collective-permute-start | bytes 103688 | tf_op jit(solution)/shard_map/ppermute | solution.py:19
  3.5 14.7 %collective-permute-start = (bf16[3,960,6]{1,2,0:T(8,128)(2,1)S(1)}, bf16[3,960,6]{1,2,0:T(8,128)(2,1)S(1)}, u32[]{:S(2)}, u32[]{:S(2)}) collective-permute-start(bf16[3,960,6]{1,2,0:T(8,128)(2,1)S(1)} %copy.47), channel_id=1, source_target_pairs={{0,1},{1,2},{2,3},{3,4},{4,5},{5,6},{6,7},{7,8},{8,9},{9,10},{10,1... | collective-permute-start | bytes 103688 | tf_op jit(solution)/shard_map/ppermute | solution.py:18
  6.9 13.0 %copy-start.2 = (bf16[960,128]{1,0:T(8,128)(2,1)S(1)}, bf16[960,128]{1,0:T(8,128)(2,1)}, u32[]{:S(2)}) copy-start(bf16[960,128]{1,0:T(8,128)(2,1)} %param.7) | copy-start | bytes 737284
  6.9 13.0 %copy-start.3 = (bf16[960,128]{1,0:T(8,128)(2,1)S(1)}, bf16[960,128]{1,0:T(8,128)(2,1)}, u32[]{:S(2)}) copy-start(bf16[960,128]{1,0:T(8,128)(2,1)} %param.6) | copy-start | bytes 737284
  6.9 13.0 %copy-start.4 = (bf16[960,128]{1,0:T(8,128)(2,1)S(1)}, bf16[960,128]{1,0:T(8,128)(2,1)}, u32[]{:S(2)}) copy-start(bf16[960,128]{1,0:T(8,128)(2,1)} %param.5) | copy-start | bytes 737284
  19.9 2.6 %copy-start.13 = (f32[3,960]{1,0:T(4,128)S(1)}, f32[3,960]{1,0:T(4,128)}, u32[]{:S(2)}) copy-start(f32[3,960]{1,0:T(4,128)} %get-tuple-element.40) | copy-start | bytes 34564
  19.9 2.6 %copy-start.14 = (f32[3,960]{1,0:T(4,128)S(1)}, f32[3,960]{1,0:T(4,128)}, u32[]{:S(2)}) copy-start(f32[3,960]{1,0:T(4,128)} %get-tuple-element.41) | copy-start | bytes 34564
  19.9 2.6 %copy-start.15 = (f32[3,960]{1,0:T(4,128)S(1)}, f32[3,960]{1,0:T(4,128)}, u32[]{:S(2)}) copy-start(f32[3,960]{1,0:T(4,128)} %get-tuple-element.44) | copy-start | bytes 34564
  19.9 2.6 %copy-start.16 = (f32[3,960]{1,0:T(4,128)S(1)}, f32[3,960]{1,0:T(4,128)}, u32[]{:S(2)}) copy-start(f32[3,960]{1,0:T(4,128)} %get-tuple-element.45) | copy-start | bytes 34564
  19.9 2.6 %copy-start.17 = (f32[3,960]{1,0:T(4,128)S(1)}, f32[3,960]{1,0:T(4,128)}, u32[]{:S(2)}) copy-start(f32[3,960]{1,0:T(4,128)} %get-tuple-element.42) | copy-start | bytes 34564
  19.9 2.6 %copy-start.18 = (f32[3,960]{1,0:T(4,128)S(1)}, f32[3,960]{1,0:T(4,128)}, u32[]{:S(2)}) copy-start(f32[3,960]{1,0:T(4,128)} %get-tuple-element.43) | copy-start | bytes 34564
  19.9 2.6 %copy-start.20 = (f32[3,960,1]{1,0,2:T(4,128)S(1)}, f32[3,960,1]{1,0,2:T(4,128)}, u32[]{:S(2)}) copy-start(f32[3,960,1]{1,0,2:T(4,128)} %copy.139) | copy-start | bytes 34564
  22.5 6.4 %copy-start.9 = (f32[3,960]{1,0:T(4,128)S(1)}, f32[3,960]{1,0:T(4,128)}, u32[]{:S(2)}) copy-start(f32[3,960]{1,0:T(4,128)} %get-tuple-element.38) | copy-start | bytes 34564
  22.5 6.4 %copy-start.10 = (f32[3,960]{1,0:T(4,128)S(1)}, f32[3,960]{1,0:T(4,128)}, u32[]{:S(2)}) copy-start(f32[3,960]{1,0:T(4,128)} %get-tuple-element.39) | copy-start | bytes 34564
  22.6 6.4 %copy-start.11 = (f32[3,960]{1,0:T(4,128)S(1)}, f32[3,960]{1,0:T(4,128)}, u32[]{:S(2)}) copy-start(f32[3,960]{1,0:T(4,128)} %get-tuple-element.36) | copy-start | bytes 34564
  22.6 6.4 %copy-start.12 = (f32[3,960]{1,0:T(4,128)S(1)}, f32[3,960]{1,0:T(4,128)}, u32[]{:S(2)}) copy-start(f32[3,960]{1,0:T(4,128)} %get-tuple-element.37) | copy-start | bytes 34564
  22.6 6.4 %copy-start.19 = (f32[3,960,1]{1,0,2:T(4,128)S(1)}, f32[3,960,1]{1,0,2:T(4,128)}, u32[]{:S(2)}) copy-start(f32[3,960,1]{1,0,2:T(4,128)} %copy.140) | copy-start | bytes 34564
  27.1 1.1 %copy-start = (f32[3,960,128]{2,1,0:T(8,128)}, f32[3,960,128]{2,1,0:T(8,128)S(1)}, u32[]{:S(2)}) copy-start(f32[3,960,128]{2,1,0:T(8,128)S(1)} %fusion.31) | copy-start | bytes 4423684
  33.3 1.1 %copy-start.1 = (f32[3,960,128]{2,1,0:T(8,128)}, f32[3,960,128]{2,1,0:T(8,128)S(1)}, u32[]{:S(2)}) copy-start(f32[3,960,128]{2,1,0:T(8,128)S(1)} %fusion.25) | copy-start | bytes 4423684
  35.8 21.7 %all-to-all-start = ((bf16[2,960,128]{2,0,1:T(2,128)(2,1)}), bf16[2,960,128]{2,0,1:T(2,128)(2,1)S(1)}, u32[]{:S(2)}, u32[]{:S(2)}) async-start(bf16[2,960,128]{2,0,1:T(2,128)(2,1)} %copy.53), calls=%async_computation | async-start | bytes 983040 | tf_op jit(solution)/shard_map/all_to_all | solution.py:96
  66.3 0.9 copy-start.6
  66.4 1.0 copy-start.7
where the time goes:
time: 103 us; the launch traced here: 102 us
  local copies, waits for them, and re-layouts  26.3 us (26%)
  other arithmetic  20.2 us (20%)
  blocking collectives  17.7 us (17%)
  matrix products  14.7 us (14%)
  starting transfers between devices  12.5 us (12%)
  waiting for transfers between devices  10.4 us (10%)
    unnamed x67, local copies, waits for them, and re-layouts  19.2 us
    all_to_all x1, blocking collectives, on_device(): lax.all_to_all(convolved, 'ctx', split_axis=2, concat_axis=1, tiled=True)  17.7 us
    all_to_all x1, waiting for transfers between devices, on_device(): lax.all_to_all(outgoing, 'ctx', split_axis=1, concat_axis=2, tiled=True)  10.4 us
    all_to_all x1, starting transfers between devices, on_device(): lax.all_to_all(outgoing, 'ctx', split_axis=1, concat_axis=2, tiled=True)  8.13 us
    dot_general x2, matrix products, forward(): jnp.einsum('...cfb,cdbk->...dfk', twist, inner_fwd, precision=precise)  6.97 us
    add x1, other arithmetic, on_device(): anticausal + mirrored_taps[:, :, offset, None] * padded[:, :, later:later...  4.54 us
    dot_general x1, matrix products, inverse(): jnp.einsum('...cfk,cdkb->...dfb', spectrum, inner_inv, precision=precise)  4.47 us
    add x1, other arithmetic, on_device(): causal + short_taps[:, :, offset, None] * padded[:, :, begin:begin + tokens]  4.31 us
  transfers between devices with their start and end apart: 3, of which 1 were waited for; matrix products, arithmetic and copies ran while one was open for 15% of the time, Pallas kernels for 0%

commit v1 on v0

--- a/solution.py
+++ b/solution.py
@@ -6,6 +6,17 @@
 
 TAPS = 7
 precise = lax.Precision.HIGH
+
+
+def in_blocks(shard, dim, size):
+    before, after = (shard.shape[:dim], shard.shape[dim + 1 :])
+    return jnp.moveaxis(shard.reshape(*before, size, -1, *after), dim, 0)
+
+
+def joined_along(blocks, dim):
+    shape = list(blocks.shape[1:])
+    shape[dim] *= blocks.shape[0]
+    return jnp.moveaxis(blocks, 0, dim).reshape(shape)
 
 
 def with_halo(value, sides, width):
@@ -93,7 +104,14 @@
     product_b = (anticausal[1] * anticausal[2]).astype(jnp.bfloat16)
     tables = fourier_tables(long_filter.shape[1])
     outgoing = jnp.stack([product_a, product_b[::-1]])
-    channel_rows = lax.all_to_all(outgoing, "ctx", split_axis=1, concat_axis=2, tiled=True)
+    peers, position = (lax.axis_size("ctx"), lax.axis_index("ctx"))
+    blocks = in_blocks(outgoing, 1, peers)
+    outs = [blocks[position]]
+    for step in range(1, peers):
+        sent = blocks[position ^ step]
+        outs.append(lax.ppermute(sent, "ctx", [(i_2, i_2 ^ step) for i_2 in range(peers)]))
+    blocks = jnp.stack(outs)[position ^ jnp.arange(peers)]
+    channel_rows = joined_along(blocks, 2)
     filter_spec = forward(long_filter.astype(jnp.float32), tables)
     data_spec = forward(channel_rows.astype(jnp.float32), tables)
     filter_real = filter_spec[:, 0]

time: 103 us -> 125 us (1.21)
  starting transfers between devices: 12.5 us -> 28.8 us
  local copies, waits for them, and re-layouts: 26.3 us -> 32.8 us
  waiting for transfers between devices: 10.4 us -> 4.95 us
  other arithmetic: 20.2 us -> 23.5 us
    ppermute x0 -> x15, starting transfers between devices: none -> 24.5 us  [on_device(): lax.ppermute(sent, 'ctx', [(i_2, i_2 ^ step) for i_2 in range(peers)])]
    all_to_all x1 -> x0, waiting for transfers between devices: 10.4 us -> none  [on_device(): lax.all_to_all(outgoing, 'ctx', split_axis=1, concat_axis=2, tiled=True)]
    all_to_all x1 -> x0, starting transfers between devices: 8.13 us -> none  [on_device(): lax.all_to_all(outgoing, 'ctx', split_axis=1, concat_axis=2, tiled=True)]
    ppermute x0 -> x15, waiting for transfers between devices: none -> 4.94 us  [on_device(): lax.ppermute(sent, 'ctx', [(i_2, i_2 ^ step) for i_2 in range(peers)])]
    rev x1, local copies, waits for them, and re-layouts: 0.6 us -> 4.31 us  [on_device(): outgoing = jnp.stack([product_a, product_b[::-1]])]
    add x1, other arithmetic: 4.31 us -> 6.07 us  [on_device(): causal + short_taps[:, :, offset, None] * padded[:, :, begin:begin + tokens]]
    gather x0 -> x1, local copies, waits for them, and re-layouts: none -> 1.66 us  [on_device(): blocks = jnp.stack(outs)[position ^ jnp.arange(peers)]]
    dot_general x2, matrix products: 6.97 us -> 8.33 us  [forward(): jnp.einsum('...cfb,cdbk->...dfk', twist, inner_fwd, precision=precise)]
  transfers between devices with their start and end apart: 3 -> 17, of which waited for: 1 -> 2; matrix products, arithmetic and copies ran while one was open for 15% -> 14% of each run, Pallas kernels for 0% -> 0%
where the time goes in v1:
time: 125 us; the launch traced here: 123 us
  local copies, waits for them, and re-layouts  32.8 us (26%)
  starting transfers between devices  28.8 us (23%)
  other arithmetic  23.5 us (19%)
  blocking collectives  16.5 us (13%)
  matrix products  15.8 us (13%)
  waiting for transfers between devices  4.95 us (4%)
    ppermute x15, starting transfers between devices, on_device(): lax.ppermute(sent, 'ctx', [(i_2, i_2 ^ step) for i_2 in range(peers)])  24.5 us
    unnamed x85, local copies, waits for them, and re-layouts  19.2 us
    all_to_all x1, blocking collectives, on_device(): lax.all_to_all(convolved, 'ctx', split_axis=2, concat_axis=1, tiled=True)  16.5 us
    dot_general x2, matrix products, forward(): jnp.einsum('...cfb,cdbk->...dfk', twist, inner_fwd, precision=precise)  8.33 us
    add x1, other arithmetic, on_device(): causal + short_taps[:, :, offset, None] * padded[:, :, begin:begin + tokens]  6.07 us
    ppermute x15, waiting for transfers between devices, on_device(): lax.ppermute(sent, 'ctx', [(i_2, i_2 ^ step) for i_2 in range(peers)])  4.94 us
    add x1, other arithmetic, on_device(): anticausal + mirrored_taps[:, :, offset, None] * padded[:, :, later:later...  4.54 us
    rev x1, local copies, waits for them, and re-layouts, on_device(): outgoing = jnp.stack([product_a, product_b[::-1]])  4.31 us
  transfers between devices with their start and end apart: 17, of which 2 were waited for; matrix products, arithmetic and copies ran while one was open for 14% of the time, Pallas kernels for 0%

profile of v1, /device:TPU:0, one launch (start us, length us, event | category | flops | bytes accessed | tf_op | source)
XLA Modules:
  0.0 123.4 jit_solution(13612753143195840623)
XLA Ops:
  0.0 1.3 %pad_maximum_fusion.2 = bf16[3,960,128]{2,1,0:T(8,128)(2,1)S(1)} fusion(bf16[1,960,128]{2,1,0:T(8,128)(2,1)} %bitcast.260, bf16[1,960,128]{2,1,0:T(8,128)(2,1)} %bitcast.264, bf16[1,960,128]{2,1,0:T(8,128)(2,1)} %bitcast.268), kind=kLoop, calls=%fused_computation.56 | loop fusion | flops 737280 | bytes 1474560 | tf_op jit(solution)/shard_map/stack | solution.py:91
  1.3 0.3 fusion.95
  1.6 0.3 copy.81
  1.9 1.3 %collective-permute-start.1 = (bf16[3,960,6]{1,2,0:T(8,128)(2,1)S(1)}, bf16[3,960,6]{1,2,0:T(8,128)(2,1)S(1)}, u32[]{:S(2)}, u32[]{:S(2)}) collective-permute-start(bf16[3,960,6]{1,2,0:T(8,128)(2,1)S(1)} %copy.81), channel_id=1, source_target_pairs={{1,0},{2,1},{3,2},{4,3},{5,4},{6,5},{7,6},{8,7},{9,8},{10,9},{11,1... | collective-permute-start | bytes 103688 | tf_op jit(solution)/shard_map/ppermute | solution.py:30
  3.2 0.3 copy.77
  3.5 3.0 %collective-permute-start = (bf16[3,960,6]{1,2,0:T(8,128)(2,1)S(1)}, bf16[3,960,6]{1,2,0:T(8,128)(2,1)S(1)}, u32[]{:S(2)}, u32[]{:S(2)}) collective-permute-start(bf16[3,960,6]{1,2,0:T(8,128)(2,1)S(1)} %copy.77), channel_id=1, source_target_pairs={{0,1},{1,2},{2,3},{3,4},{4,5},{5,6},{6,7},{7,8},{8,9},{9,10},{10,1... | collective-permute-start | bytes 103688 | tf_op jit(solution)/shard_map/ppermute | solution.py:29
  7.3 0.7 reverse.8
  8.2 0.7 reverse.7
  9.0 0.7 reverse.12
  9.9 0.7 reverse.11
  10.7 0.7 reverse.10
  11.5 0.6 copy_bitcast_fusion.24
  12.2 0.7 reverse.9
  13.0 0.6 copy_bitcast_fusion.15
  13.6 0.6 copy_bitcast_fusion.19
  14.3 0.6 copy_bitcast_fusion.17
  14.9 0.7 convolution_bitcast_fusion.1
  15.6 0.3 multiply_add_fusion.4
  16.1 0.7 fusion.60
  16.8 3.4 %fusion.17 = f32[60,2,32,128]{3,0,2,1:T(8,128)} fusion(f32[60,2,32,128]{3,2,0,1:T(8,128)S(1)} %pad_maximum_fusion, f32[1,2,128,128]{3,2,0,1:T(8,128)S(1)} %get-tuple-element.38, f32[1,2,128,128]{3,2,0,1:T(8,128)S(1)} %get-tuple-element.48), kind=kOutput, calls=%fused_computation.26 | convolution fusion | flops 755040256 | bytes 4194304 | tf_op jit(solution)/shard_map/...cfb,cdbk->...dfk/dot_general | solution.py:68
  20.2 0.6 pad_clamp_fusion
  20.8 0.6 copy.216
  21.4 0.7 reverse.13
  22.2 0.6 copy.215
  22.9 0.4 copy.78
  23.3 1.2 copy.82
  24.6 2.6 %maximum_maximum_fusion = (bf16[3,960,134]{2,1,0:T(8,128)(2,1)S(1)}, bf16[3,960,134]{2,1,0:T(8,128)(2,1)S(1)}) fusion(bf16[1,960,128]{2,1,0:T(8,128)(2,1)S(1)} %bitcast.261, bf16[1,960,128]{2,1,0:T(8,128)(2,1)S(1)} %bitcast.265, bf16[1,960,128]{2,1,0:T(8,128)(2,1)S(1)} %bitcast.270, bf16[3,960,6]{2,1,0:T(8,128)(2,1)S(1)} %copy.78, bf16[3,960,6]{2,1,0:T(8,128)(2,1)} %copy.82), kind=kLoop, calls=%fused_computation.40 | loop fusion | flops 6174720 | bytes 2350080 | tf_op jit(solution)/shard_map/concatenate | solution.py:31
  27.3 4.5 %fusion.31 = f32[3,960,128]{2,1,0:T(8,128)S(1)} fusion(bf16[3,960,134]{2,1,0:T(8,128)(2,1)S(1)} %get-tuple-element.16, f32[3,960]{1,0:T(4,128)S(1)} %copy-done.15, f32[3,960]{1,0:T(4,128)S(1)} %copy-done.16, f32[3,960]{1,0:T(4,128)S(1)} %copy-done.19, f32[3,960]{1,0:T(4,128)S(1)} %copy-done.20, f32[3,960]{1,0:T(4,128)S(1)} %copy-done.17, ...), kind=kLoop, calls=%fused_computation.39 | loop fusion | flops 8110080 | bytes 6716160 | tf_op jit(solution)/shard_map/add | solution.py:101
  31.8 0.7 fusion.55
  32.6 4.3 %rev.7 = bf16[960,128]{1,0:T(8,128)(2,1)} reverse(bf16[960,128]{1,0:T(8,128)(2,1)} %fusion.55), dimensions={0} | reverse | bytes 491520 | tf_op jit(solution)/shard_map/rev | solution.py:106
  36.9 1.7 %stack.163 = bf16[1,16,60,128]{3,2,1,0:T(8,128)(2,1)} reshape(bf16[960,128]{1,0:T(8,128)(2,1)} %rev.7) | data formatting | bytes 491520 | tf_op jit(solution)/shard_map/stack | solution.py:106
  38.6 6.1 %fusion.25 = f32[3,960,128]{2,1,0:T(8,128)S(1)} fusion(bf16[3,960,134]{2,1,0:T(8,128)(2,1)S(1)} %get-tuple-element.15, f32[3,960]{1,0:T(4,128)S(1)} %get-tuple-element.50, f32[3,960]{1,0:T(4,128)S(1)} %get-tuple-element.51, f32[3,960]{1,0:T(4,128)} %get-tuple-element.52, f32[3,960]{1,0:T(4,128)} %get-tuple-element.53, f32[3,960]{1,0:T(4,128)S(1)} %get-tuple-element.54, ...), kind=kLoop, calls=%fused_computation.33 | loop fusion | flops 8110080 | bytes 6716160 | tf_op jit(solution)/shard_map/add | solution.py:98
  44.7 1.1 copy-done.1
  45.9 0.8 copy-done.10
  47.2 2.7 %collective-permute-start.2 = (bf16[2,60,128]{2,0,1:T(2,128)(2,1)S(1)}, bf16[2,60,128]{2,0,1:T(2,128)(2,1)S(1)}, u32[]{:S(2)}, u32[]{:S(2)}) collective-permute-start(bf16[2,60,128]{2,0,1:T(2,128)(2,1)S(1)} %bitcast.299), channel_id=1, source_target_pairs={{0,1},{1,0},{2,3},{3,2},{4,5},{5,4},{6,7},{7,6},{8,9},{9,8},{10,11... | collective-permute-start | bytes 92168 | tf_op jit(solution)/shard_map/ppermute | solution.py:112
  49.8 2.4 %collective-permute-start.3 = (bf16[2,60,128]{2,0,1:T(2,128)(2,1)S(1)}, bf16[2,60,128]{2,0,1:T(2,128)(2,1)S(1)}, u32[]{:S(2)}, u32[]{:S(2)}) collective-permute-start(bf16[2,60,128]{2,0,1:T(2,128)(2,1)S(1)} %bitcast.297), channel_id=1, source_target_pairs={{0,2},{1,3},{2,0},{3,1},{4,6},{5,7},{6,4},{7,5},{8,10},{9,11},{10,... | collective-permute-start | bytes 92168 | tf_op jit(solution)/shard_map/ppermute | solution.py:112
  52.2 1.6 %collective-permute-start.5 = (bf16[2,60,128]{2,0,1:T(2,128)(2,1)S(1)}, bf16[2,60,128]{2,0,1:T(2,128)(2,1)S(1)}, u32[]{:S(2)}, u32[]{:S(2)}) collective-permute-start(bf16[2,60,128]{2,0,1:T(2,128)(2,1)S(1)} %bitcast.293), channel_id=1, source_target_pairs={{0,4},{1,5},{2,6},{3,7},{4,0},{5,1},{6,2},{7,3},{8,12},{9,13},{10,... | collective-permute-start | bytes 92168 | tf_op jit(solution)/shard_map/ppermute | solution.py:112
  54.2 3.0 %collective-permute-start.7 = (bf16[2,60,128]{2,0,1:T(2,128)(2,1)S(1)}, bf16[2,60,128]{2,0,1:T(2,128)(2,1)S(1)}, u32[]{:S(2)}, u32[]{:S(2)}) collective-permute-start(bf16[2,60,128]{2,0,1:T(2,128)(2,1)S(1)} %bitcast.298), channel_id=1, source_target_pairs={{0,6},{1,7},{2,4},{3,5},{4,2},{5,3},{6,0},{7,1},{8,14},{9,15},{10,... | collective-permute-start | bytes 92168 | tf_op jit(solution)/shard_map/ppermute | solution.py:112
  57.4 2.5 %collective-permute-start.9 = (bf16[2,60,128]{2,0,1:T(2,128)(2,1)S(1)}, bf16[2,60,128]{2,0,1:T(2,128)(2,1)S(1)}, u32[]{:S(2)}, u32[]{:S(2)}) collective-permute-start(bf16[2,60,128]{2,0,1:T(2,128)(2,1)S(1)} %bitcast.294), channel_id=1, source_target_pairs={{0,8},{1,9},{2,10},{3,11},{4,12},{5,13},{6,14},{7,15},{8,0},{9,1},... | collective-permute-start | bytes 92168 | tf_op jit(solution)/shard_map/ppermute | solution.py:112
  60.1 3.9 %collective-permute-start.11 = (bf16[2,60,128]{2,0,1:T(2,128)(2,1)S(1)}, bf16[2,60,128]{2,0,1:T(2,128)(2,1)S(1)}, u32[]{:S(2)}, u32[]{:S(2)}) collective-permute-start(bf16[2,60,128]{2,0,1:T(2,128)(2,1)S(1)} %bitcast.290), channel_id=1, source_target_pairs={{0,10},{1,11},{2,8},{3,9},{4,14},{5,15},{6,12},{7,13},{8,2},{9,3},... | collective-permute-start | bytes 92168 | tf_op jit(solution)/shard_map/ppermute | solution.py:112
  64.1 2.5 %collective-permute-start.13 = (bf16[2,60,128]{2,0,1:T(2,128)(2,1)S(1)}, bf16[2,60,128]{2,0,1:T(2,128)(2,1)S(1)}, u32[]{:S(2)}, u32[]{:S(2)}) collective-permute-start(bf16[2,60,128]{2,0,1:T(2,128)(2,1)S(1)} %bitcast.288), channel_id=1, source_target_pairs={{0,12},{1,13},{2,14},{3,15},{4,8},{5,9},{6,10},{7,11},{8,4},{9,5},... | collective-permute-start | bytes 92168 | tf_op jit(solution)/shard_map/ppermute | solution.py:112
  66.7 0.9 collective-permute-start.14
  67.6 3.6 %collective-permute-start.15 = (bf16[2,60,128]{2,0,1:T(2,128)(2,1)S(1)}, bf16[2,60,128]{2,0,1:T(2,128)(2,1)S(1)}, u32[]{:S(2)}, u32[]{:S(2)}) collective-permute-start(bf16[2,60,128]{2,0,1:T(2,128)(2,1)S(1)} %bitcast.286), channel_id=1, source_target_pairs={{0,14},{1,15},{2,12},{3,13},{4,10},{5,11},{6,8},{7,9},{8,6},{9,7},... | collective-permute-start | bytes 92168 | tf_op jit(solution)/shard_map/ppermute | solution.py:112
  71.3 1.3 %collective-permute-start.16 = (bf16[2,60,128]{2,0,1:T(2,128)(2,1)S(1)}, bf16[2,60,128]{2,0,1:T(2,128)(2,1)S(1)}, u32[]{:S(2)}, u32[]{:S(2)}) collective-permute-start(bf16[2,60,128]{2,0,1:T(2,128)(2,1)S(1)} %bitcast.285), channel_id=1, source_target_pairs={{0,15},{1,14},{2,13},{3,12},{4,11},{5,10},{6,9},{7,8},{8,7},{9,6},... | collective-permute-start | bytes 92168 | tf_op jit(solution)/shard_map/ppermute | solution.py:112
  72.7 1.7 %collective-permute-done.15 = bf16[2,60,128]{2,0,1:T(2,128)(2,1)S(1)} collective-permute-done((bf16[2,60,128]{2,0,1:T(2,128)(2,1)S(1)}, bf16[2,60,128]{2,0,1:T(2,128)(2,1)S(1)}, u32[]{:S(2)}, u32[]{:S(2)}) %collective-permute-start.15) | collective-permute-done | bytes 30752 | tf_op jit(solution)/shard_map/ppermute | solution.py:112
  74.4 3.2 %collective-permute-done.16 = bf16[2,60,128]{2,0,1:T(2,128)(2,1)S(1)} collective-permute-done((bf16[2,60,128]{2,0,1:T(2,128)(2,1)S(1)}, bf16[2,60,128]{2,0,1:T(2,128)(2,1)S(1)}, u32[]{:S(2)}, u32[]{:S(2)}) %collective-permute-start.16) | collective-permute-done | bytes 30752 | tf_op jit(solution)/shard_map/ppermute | solution.py:112
  77.7 1.7 %gather_fusion = bf16[16,2,60,128]{3,1,2,0:T(2,128)(2,1)S(1)} fusion(bf16[16,2,60,128]{3,1,2,0:T(2,128)(2,1)S(1)} %constant_dynamic-update-slice_fusion.2, s32[1024]{0:T(1024)} %pad_clamp_fusion), kind=kCustom, calls=%fused_computation | custom fusion | bytes 983104 | tf_op jit(solution)/shard_map/gather | solution.py:113
  79.4 1.2 convolution_bitcast_fusion
  80.6 0.8 multiply_add_fusion.1
  81.4 0.4 maximum_bitcast_fusion.1
  81.8 0.5 copy-done.7
  82.4 5.0 %fusion.8 = f32[2,60,2,32,128]{4,1,3,2,0:T(8,128)S(1)} fusion(f32[2,60,2,32,128,1]{4,3,1,0,2,5:T(8,128)S(1)} %maximum_bitcast_fusion.1, f32[1,2,128,128]{3,2,0,1:T(8,128)S(1)} %copy-done.7, f32[1,2,128,128]{3,2,0,1:T(8,128)S(1)} %copy-done.9), kind=kOutput, calls=%fused_computation.11 | convolution fusion | flops 1510014976 | bytes 8126464 | tf_op jit(solution)/shard_map/...cfb,cdbk->...dfk/dot_general | solution.py:68
  87.3 1.2 multiply_subtract_fusion.3
  89.2 0.4 maximum_bitcast_fusion
  89.9 4.3 %fusion.14 = f32[2,60,2,32,128]{4,3,1,0,2:T(8,128)S(1)} fusion(f32[2,60,2,32,128,1]{4,1,3,2,0,5:T(8,128)S(1)} %maximum_bitcast_fusion, f32[1,2,128,128]{3,2,1,0:T(8,128)S(1)} %copy-done.13, f32[1,2,128,128]{3,2,1,0:T(8,128)S(1)} %copy-done.12), kind=kOutput, calls=%fused_computation.17 | convolution fusion | flops 1510014976 | bytes 8126464 | tf_op jit(solution)/shard_map/...cfk,cdkb->...dfb/dot_general | solution.py:73
  94.2 0.6 multiply_subtract_fusion
  94.8 1.3 %fusion.41 = bf16[2,60,16,128]{3,2,1,0:T(8,128)(2,1)S(1)} fusion(f32[2,60,1,32,128]{4,3,1,0,2:T(8,128)S(1)} %get-tuple-element.10, f32[2,60,1,32,128]{4,3,1,0,2:T(8,128)S(1)} %get-tuple-element.9, f32[1,16,32]{2,1,0:T(8,128)S(1)} %get-tuple-element.62, f32[1,16,32]{2,1,0:T(8,128)S(1)} %get-tuple-element.63), kind=kOutput, calls=%fused_computation.45 | convolution fusion | flops 95847424 | bytes 4427776 | tf_op jit(solution)/shard_map/...cfb,caf->...ab/dot_general | solution.py:83
  96.1 0.8 copy.134
  96.9 2.8 %reshape.285 = bf16[16,2,7680]{2,1,0:T(2,128)(2,1)S(1)} reshape(bf16[2048,2,60]{2,1,0:T(2,128)(2,1)S(1)} %bitcast.258) | data formatting | bytes 983040
  99.7 16.5 %all_to_all.15 = bf16[16,2,7680]{2,1,0:T(2,128)(2,1)S(1)} all-to-all(bf16[16,2,7680]{2,1,0:T(2,128)(2,1)S(1)} %reshape.285), channel_id=1, replica_groups=mesh['grp'=2,'ctx'=16] {'ctx'}, dimensions={0} | all-to-all | bytes 983040 | tf_op jit(solution)/shard_map/all_to_all | solution.py:129
  116.2 3.5 %reshape.286 = bf16[2048,2,60]{2,1,0:T(2,128)(2,1)S(1)} reshape(bf16[16,2,7680]{2,1,0:T(2,128)(2,1)S(1)} %all_to_all.15) | data formatting | bytes 983040
  119.7 0.8 copy.133
  120.8 0.6 rev.8
  121.6 1.8 %fusion.46 = bf16[960,128]{1,0:T(8,128)(2,1)} fusion(f32[3,960,128]{2,1,0:T(8,128)S(1)} %fusion.31, f32[960,128]{1,0:T(8,128)S(1)} %reshape.260, f32[3,960,128]{2,1,0:T(8,128)} %copy-done.1, bf16[960,128]{1,0:T(8,128)(2,1)S(1)} %rev.8), kind=kLoop, calls=%fused_computation.60 | loop fusion | flops 614400 | bytes 1966080 | tf_op jit(solution)/shard_map/convert_element_type | solution.py:134
  (121 shorter events, 4.4 us)
Async XLA Ops:
  1.3 6.0 %copy-start.14 = (f32[3,960,7]{1,2,0:T(8,128)S(1)}, f32[3,960,7]{1,2,0:T(8,128)}, u32[]{:S(2)}) copy-start(f32[3,960,7]{1,2,0:T(8,128)} %param.8) | copy-start | bytes 241924
  1.6 11.4 %copy-start.11 = (bf16[60,2048]{1,0:T(8,128)(2,1)S(1)}, bf16[60,2048]{1,0:T(8,128)(2,1)}, u32[]{:S(2)}) copy-start(bf16[60,2048]{1,0:T(8,128)(2,1)} %param.9) | copy-start | bytes 737284
  1.9 21.4 %collective-permute-start.1 = (bf16[3,960,6]{1,2,0:T(8,128)(2,1)S(1)}, bf16[3,960,6]{1,2,0:T(8,128)(2,1)S(1)}, u32[]{:S(2)}, u32[]{:S(2)}) collective-permute-start(bf16[3,960,6]{1,2,0:T(8,128)(2,1)S(1)} %copy.81), channel_id=1, source_target_pairs={{1,0},{2,1},{3,2},{4,3},{5,4},{6,5},{7,6},{8,7},{9,8},{10,9},{11,1... | collective-permute-start | bytes 103688 | tf_op jit(solution)/shard_map/ppermute | solution.py:30
  3.5 19.4 %collective-permute-start = (bf16[3,960,6]{1,2,0:T(8,128)(2,1)S(1)}, bf16[3,960,6]{1,2,0:T(8,128)(2,1)S(1)}, u32[]{:S(2)}, u32[]{:S(2)}) collective-permute-start(bf16[3,960,6]{1,2,0:T(8,128)(2,1)S(1)} %copy.77), channel_id=1, source_target_pairs={{0,1},{1,2},{2,3},{3,4},{4,5},{5,6},{6,7},{7,8},{8,9},{9,10},{10,1... | collective-permute-start | bytes 103688 | tf_op jit(solution)/shard_map/ppermute | solution.py:29
  16.8 3.4 %copy-start.6 = (f32[1,2,128,128]{3,2,0,1:T(8,128)}, f32[1,2,128,128]{3,2,0,1:T(8,128)S(1)}, u32[]{:S(2)}) copy-start(f32[1,2,128,128]{3,2,0,1:T(8,128)S(1)} %get-tuple-element.38) | copy-start | bytes 393220
  16.8 3.4 %copy-start.8 = (f32[1,2,128,128]{3,2,0,1:T(8,128)}, f32[1,2,128,128]{3,2,0,1:T(8,128)S(1)}, u32[]{:S(2)}) copy-start(f32[1,2,128,128]{3,2,0,1:T(8,128)S(1)} %get-tuple-element.48) | copy-start | bytes 393220
  20.2 4.3 %copy-start.2 = (bf16[960,128]{1,0:T(8,128)(2,1)S(1)}, bf16[960,128]{1,0:T(8,128)(2,1)}, u32[]{:S(2)}) copy-start(bf16[960,128]{1,0:T(8,128)(2,1)} %param.7) | copy-start | bytes 737284
  20.2 4.3 %copy-start.3 = (bf16[960,128]{1,0:T(8,128)(2,1)S(1)}, bf16[960,128]{1,0:T(8,128)(2,1)}, u32[]{:S(2)}) copy-start(bf16[960,128]{1,0:T(8,128)(2,1)} %param.6) | copy-start | bytes 737284
  20.2 4.3 %copy-start.4 = (bf16[960,128]{1,0:T(8,128)(2,1)S(1)}, bf16[960,128]{1,0:T(8,128)(2,1)}, u32[]{:S(2)}) copy-start(bf16[960,128]{1,0:T(8,128)(2,1)} %param.5) | copy-start | bytes 737284
  24.5 2.7 %copy-start.5 = (bf16[960,128]{1,0:T(8,128)(2,1)S(1)}, bf16[960,128]{1,0:T(8,128)(2,1)}, u32[]{:S(2)}) copy-start(bf16[960,128]{1,0:T(8,128)(2,1)} %param.5) | copy-start | bytes 737284
  24.5 2.7 %copy-start.15 = (f32[3,960]{1,0:T(4,128)S(1)}, f32[3,960]{1,0:T(4,128)}, u32[]{:S(2)}) copy-start(f32[3,960]{1,0:T(4,128)} %get-tuple-element.56) | copy-start | bytes 34564
  24.5 2.7 %copy-start.16 = (f32[3,960]{1,0:T(4,128)S(1)}, f32[3,960]{1,0:T(4,128)}, u32[]{:S(2)}) copy-start(f32[3,960]{1,0:T(4,128)} %get-tuple-element.57) | copy-start | bytes 34564
  24.5 2.7 %copy-start.17 = (f32[3,960]{1,0:T(4,128)S(1)}, f32[3,960]{1,0:T(4,128)}, u32[]{:S(2)}) copy-start(f32[3,960]{1,0:T(4,128)} %get-tuple-element.60) | copy-start | bytes 34564
  24.5 2.7 %copy-start.18 = (f32[3,960]{1,0:T(4,128)S(1)}, f32[3,960]{1,0:T(4,128)}, u32[]{:S(2)}) copy-start(f32[3,960]{1,0:T(4,128)} %get-tuple-element.61) | copy-start | bytes 34564
  24.6 2.7 %copy-start.19 = (f32[3,960]{1,0:T(4,128)S(1)}, f32[3,960]{1,0:T(4,128)}, u32[]{:S(2)}) copy-start(f32[3,960]{1,0:T(4,128)} %get-tuple-element.58) | copy-start | bytes 34564
  24.6 2.7 %copy-start.20 = (f32[3,960]{1,0:T(4,128)S(1)}, f32[3,960]{1,0:T(4,128)}, u32[]{:S(2)}) copy-start(f32[3,960]{1,0:T(4,128)} %get-tuple-element.59) | copy-start | bytes 34564
  24.6 2.7 %copy-start.21 = (f32[3,960,1]{1,0,2:T(4,128)S(1)}, f32[3,960,1]{1,0,2:T(4,128)}, u32[]{:S(2)}) copy-start(f32[3,960,1]{1,0,2:T(4,128)} %copy.215) | copy-start | bytes 34564
  44.7 1.1 copy-start.1
  45.8 0.9 copy-start.10
  47.2 7.0 %collective-permute-start.2 = (bf16[2,60,128]{2,0,1:T(2,128)(2,1)S(1)}, bf16[2,60,128]{2,0,1:T(2,128)(2,1)S(1)}, u32[]{:S(2)}, u32[]{:S(2)}) collective-permute-start(bf16[2,60,128]{2,0,1:T(2,128)(2,1)S(1)} %bitcast.299), channel_id=1, source_target_pairs={{0,1},{1,0},{2,3},{3,2},{4,5},{5,4},{6,7},{7,6},{8,9},{9,8},{10,11... | collective-permute-start | bytes 92168 | tf_op jit(solution)/shard_map/ppermute | solution.py:112
  49.8 7.4 %collective-permute-start.3 = (bf16[2,60,128]{2,0,1:T(2,128)(2,1)S(1)}, bf16[2,60,128]{2,0,1:T(2,128)(2,1)S(1)}, u32[]{:S(2)}, u32[]{:S(2)}) collective-permute-start(bf16[2,60,128]{2,0,1:T(2,128)(2,1)S(1)} %bitcast.297), channel_id=1, source_target_pairs={{0,2},{1,3},{2,0},{3,1},{4,6},{5,7},{6,4},{7,5},{8,10},{9,11},{10,... | collective-permute-start | bytes 92168 | tf_op jit(solution)/shard_map/ppermute | solution.py:112
  52.2 5.2 %collective-permute-start.4 = (bf16[2,60,128]{2,0,1:T(2,128)(2,1)S(1)}, bf16[2,60,128]{2,0,1:T(2,128)(2,1)S(1)}, u32[]{:S(2)}, u32[]{:S(2)}) collective-permute-start(bf16[2,60,128]{2,0,1:T(2,128)(2,1)S(1)} %bitcast.295), channel_id=1, source_target_pairs={{0,3},{1,2},{2,1},{3,0},{4,7},{5,6},{6,5},{7,4},{8,11},{9,10},{10,... | collective-permute-start | bytes 92168 | tf_op jit(solution)/shard_map/ppermute | solution.py:112
  52.2 7.8 %collective-permute-start.5 = (bf16[2,60,128]{2,0,1:T(2,128)(2,1)S(1)}, bf16[2,60,128]{2,0,1:T(2,128)(2,1)S(1)}, u32[]{:S(2)}, u32[]{:S(2)}) collective-permute-start(bf16[2,60,128]{2,0,1:T(2,128)(2,1)S(1)} %bitcast.293), channel_id=1, source_target_pairs={{0,4},{1,5},{2,6},{3,7},{4,0},{5,1},{6,2},{7,3},{8,12},{9,13},{10,... | collective-permute-start | bytes 92168 | tf_op jit(solution)/shard_map/ppermute | solution.py:112
  53.8 6.3 %collective-permute-start.6 = (bf16[2,60,128]{2,0,1:T(2,128)(2,1)S(1)}, bf16[2,60,128]{2,0,1:T(2,128)(2,1)S(1)}, u32[]{:S(2)}, u32[]{:S(2)}) collective-permute-start(bf16[2,60,128]{2,0,1:T(2,128)(2,1)S(1)} %bitcast.291), channel_id=1, source_target_pairs={{0,5},{1,4},{2,7},{3,6},{4,1},{5,0},{6,3},{7,2},{8,13},{9,12},{10,... | collective-permute-start | bytes 92168 | tf_op jit(solution)/shard_map/ppermute | solution.py:112
  54.2 9.8 %collective-permute-start.7 = (bf16[2,60,128]{2,0,1:T(2,128)(2,1)S(1)}, bf16[2,60,128]{2,0,1:T(2,128)(2,1)S(1)}, u32[]{:S(2)}, u32[]{:S(2)}) collective-permute-start(bf16[2,60,128]{2,0,1:T(2,128)(2,1)S(1)} %bitcast.298), channel_id=1, source_target_pairs={{0,6},{1,7},{2,4},{3,5},{4,2},{5,3},{6,0},{7,1},{8,14},{9,15},{10,... | collective-permute-start | bytes 92168 | tf_op jit(solution)/shard_map/ppermute | solution.py:112
  57.3 6.8 %collective-permute-start.8 = (bf16[2,60,128]{2,0,1:T(2,128)(2,1)S(1)}, bf16[2,60,128]{2,0,1:T(2,128)(2,1)S(1)}, u32[]{:S(2)}, u32[]{:S(2)}) collective-permute-start(bf16[2,60,128]{2,0,1:T(2,128)(2,1)S(1)} %bitcast.296), channel_id=1, source_target_pairs={{0,7},{1,6},{2,5},{3,4},{4,3},{5,2},{6,1},{7,0},{8,15},{9,14},{10,... | collective-permute-start | bytes 92168 | tf_op jit(solution)/shard_map/ppermute | solution.py:112
  57.4 9.2 %collective-permute-start.9 = (bf16[2,60,128]{2,0,1:T(2,128)(2,1)S(1)}, bf16[2,60,128]{2,0,1:T(2,128)(2,1)S(1)}, u32[]{:S(2)}, u32[]{:S(2)}) collective-permute-start(bf16[2,60,128]{2,0,1:T(2,128)(2,1)S(1)} %bitcast.294), channel_id=1, source_target_pairs={{0,8},{1,9},{2,10},{3,11},{4,12},{5,13},{6,14},{7,15},{8,0},{9,1},... | collective-permute-start | bytes 92168 | tf_op jit(solution)/shard_map/ppermute | solution.py:112
  59.9 7.7 %collective-permute-start.10 = (bf16[2,60,128]{2,0,1:T(2,128)(2,1)S(1)}, bf16[2,60,128]{2,0,1:T(2,128)(2,1)S(1)}, u32[]{:S(2)}, u32[]{:S(2)}) collective-permute-start(bf16[2,60,128]{2,0,1:T(2,128)(2,1)S(1)} %bitcast.292), channel_id=1, source_target_pairs={{0,9},{1,8},{2,11},{3,10},{4,13},{5,12},{6,15},{7,14},{8,1},{9,0},... | collective-permute-start | bytes 92168 | tf_op jit(solution)/shard_map/ppermute | solution.py:112
  60.1 11.2 %collective-permute-start.11 = (bf16[2,60,128]{2,0,1:T(2,128)(2,1)S(1)}, bf16[2,60,128]{2,0,1:T(2,128)(2,1)S(1)}, u32[]{:S(2)}, u32[]{:S(2)}) collective-permute-start(bf16[2,60,128]{2,0,1:T(2,128)(2,1)S(1)} %bitcast.290), channel_id=1, source_target_pairs={{0,10},{1,11},{2,8},{3,9},{4,14},{5,15},{6,12},{7,13},{8,2},{9,3},... | collective-permute-start | bytes 92168 | tf_op jit(solution)/shard_map/ppermute | solution.py:112
  64.0 8.6 %collective-permute-start.12 = (bf16[2,60,128]{2,0,1:T(2,128)(2,1)S(1)}, bf16[2,60,128]{2,0,1:T(2,128)(2,1)S(1)}, u32[]{:S(2)}, u32[]{:S(2)}) collective-permute-start(bf16[2,60,128]{2,0,1:T(2,128)(2,1)S(1)} %bitcast.289), channel_id=1, source_target_pairs={{0,11},{1,10},{2,9},{3,8},{4,15},{5,14},{6,13},{7,12},{8,3},{9,2},... | collective-permute-start | bytes 92168 | tf_op jit(solution)/shard_map/ppermute | solution.py:112
  64.1 8.5 %collective-permute-start.13 = (bf16[2,60,128]{2,0,1:T(2,128)(2,1)S(1)}, bf16[2,60,128]{2,0,1:T(2,128)(2,1)S(1)}, u32[]{:S(2)}, u32[]{:S(2)}) collective-permute-start(bf16[2,60,128]{2,0,1:T(2,128)(2,1)S(1)} %bitcast.288), channel_id=1, source_target_pairs={{0,12},{1,13},{2,14},{3,15},{4,8},{5,9},{6,10},{7,11},{8,4},{9,5},... | collective-permute-start | bytes 92168 | tf_op jit(solution)/shard_map/ppermute | solution.py:112
  66.7 6.0 %collective-permute-start.14 = (bf16[2,60,128]{2,0,1:T(2,128)(2,1)S(1)}, bf16[2,60,128]{2,0,1:T(2,128)(2,1)S(1)}, u32[]{:S(2)}, u32[]{:S(2)}) collective-permute-start(bf16[2,60,128]{2,0,1:T(2,128)(2,1)S(1)} %bitcast.287), channel_id=1, source_target_pairs={{0,13},{1,12},{2,15},{3,14},{4,9},{5,8},{6,11},{7,10},{8,5},{9,4},... | collective-permute-start | bytes 92168 | tf_op jit(solution)/shard_map/ppermute | solution.py:112
  67.6 6.8 %collective-permute-start.15 = (bf16[2,60,128]{2,0,1:T(2,128)(2,1)S(1)}, bf16[2,60,128]{2,0,1:T(2,128)(2,1)S(1)}, u32[]{:S(2)}, u32[]{:S(2)}) collective-permute-start(bf16[2,60,128]{2,0,1:T(2,128)(2,1)S(1)} %bitcast.286), channel_id=1, source_target_pairs={{0,14},{1,15},{2,12},{3,13},{4,10},{5,11},{6,8},{7,9},{8,6},{9,7},... | collective-permute-start | bytes 92168 | tf_op jit(solution)/shard_map/ppermute | solution.py:112
  71.3 6.4 %collective-permute-start.16 = (bf16[2,60,128]{2,0,1:T(2,128)(2,1)S(1)}, bf16[2,60,128]{2,0,1:T(2,128)(2,1)S(1)}, u32[]{:S(2)}, u32[]{:S(2)}) collective-permute-start(bf16[2,60,128]{2,0,1:T(2,128)(2,1)S(1)} %bitcast.285), channel_id=1, source_target_pairs={{0,15},{1,14},{2,13},{3,12},{4,11},{5,10},{6,9},{7,8},{8,7},{9,6},... | collective-permute-start | bytes 92168 | tf_op jit(solution)/shard_map/ppermute | solution.py:112
  81.4 0.9 copy-start.7
  81.4 1.0 copy-start.9
  82.4 5.0 %copy-start = (f32[60,2,32,128]{3,0,2,1:T(8,128)S(1)}, f32[60,2,32,128]{3,0,2,1:T(8,128)}, u32[]{:S(2)}) copy-start(f32[60,2,32,128]{3,0,2,1:T(8,128)} %fusion.17) | copy-start | bytes 5898244
  88.9 0.9 copy-start.12
  88.9 1.0 copy-start.13
